TPU v7x, 128 devices: a whole 4x4x4 slice. The times are simulated.
128 devices in a mesh: ctx: 32 (over z, y, core), head: 4 (over x).
Axes of the slice: x: 4, y: 4, z: 4, core: 2. Of those that a mesh axis runs over, the one named last changes fastest.
Arguments:
- queries: bfloat16 [49152, 2048], P('ctx', 'head'), may hold values from -20 to 20
- keys: bfloat16 [49152, 2048], P('ctx', 'head'), may hold values from -20 to 20
- values: bfloat16 [49152, 2048], P('ctx', 'head'), may hold values from -6 to 6
- offsets: int32 [3, 16], replicated, may hold values from 0 to 7, as said below
- out_weight: bfloat16 [2048, 2048], replicated, may hold values from -1.1953125 to 1.1953125
Outputs:
- mixed: bfloat16 [49152, 2048], P(('ctx', 'head'))
Inputs may be any that keep to these rules, and one draw needn't show every extreme that they name: `offsets`: each offset of row k - 1 lies in 0 to 2^k - 1; in the last row every value of that range occurs.
All inputs are finite; a program needn't handle non-finite values.
Results may differ from a plain program's by a relative error of at most 0.0053.
Values may be sent and summed in bfloat16 or wider, within the bound.
A program may use at most 192 MiB of HBM per device.

v0:
```python
import math
import jax
import jax.numpy as jnp
from jax import lax
from jax.sharding import PartitionSpec as P

DH = 128
LEVELS = 4
NEG_FILL = -1e30


def swapped(value, axis, bit):
    mask = 2**bit
    pairs = [(source, source ^ mask) for source in range(lax.axis_size(axis))]
    return lax.ppermute(value, axis, pairs)


def pick_rows(source, shifts, dilation):
    hits = jnp.arange(dilation)[:, None] == shifts[None, :]
    shaped = source.reshape(source.shape[0] // dilation, dilation, source.shape[1], source.shape[2])
    return jnp.sum(jnp.where(hits[None, :, :, None], shaped, jnp.zeros((), source.dtype)), axis=1)


def block_attend(query_rows, key_rows, value_rows, query_pos):
    number = query_rows.shape[0]
    heads_here = query_rows.shape[1]
    width_head = query_rows.shape[2]
    height = 512 if number % 512 == 0 else number
    blocks = number // height
    key_pos = jnp.arange(key_rows.shape[0])
    factor = 1.0 / math.sqrt(width_head)

    def one_block(items):
        rows_now, pos_now = items
        scores = (
            jnp.einsum("qhd,khd->hqk", rows_now, key_rows, preferred_element_type=jnp.float32)
            * factor
        )
        scores = jnp.where(pos_now[None, :, None] >= key_pos[None, None, :], scores, NEG_FILL)
        row_max = jnp.max(scores, axis=2)
        weights = jnp.exp(scores - row_max[:, :, None])
        row_sum = jnp.sum(weights, axis=2)
        weighted = jnp.einsum(
            "hqk,khd->qhd",
            weights.astype(jnp.bfloat16),
            value_rows,
            preferred_element_type=jnp.float32,
        )
        return (row_max.T, row_sum.T, weighted)

    shaped_rows = query_rows.reshape(blocks, height, heads_here, width_head)
    maxima, sums_all, outputs = lax.map(one_block, (shaped_rows, query_pos.reshape(blocks, height)))
    return (
        maxima.reshape(number, heads_here),
        sums_all.reshape(number, heads_here),
        outputs.reshape(number, heads_here, width_head),
    )


def spread_rows(parts, shifts, dilation):
    row_max, row_sum, weighted = parts
    hits = jnp.arange(dilation)[:, None] == shifts[None, :]
    number = row_max.shape[0] * dilation
    heads_here = row_max.shape[1]
    full_max = jnp.where(hits[None], row_max[:, None, :], NEG_FILL).reshape(number, heads_here)
    full_sum = jnp.where(hits[None], row_sum[:, None, :], 0.0).reshape(number, heads_here)
    full_out = jnp.where(hits[None, :, :, None], weighted[:, None], 0.0).reshape(
        number, heads_here, weighted.shape[2]
    )
    return (full_max, full_sum, full_out)


def merge_levels(running, fresh):
    new_max = jnp.maximum(running[0], fresh[0])
    old_scale = jnp.exp(running[0] - new_max)
    new_scale = jnp.exp(fresh[0] - new_max)
    new_sum = running[1] * old_scale + fresh[1] * new_scale
    new_out = running[2] * old_scale[:, :, None] + fresh[2] * new_scale[:, :, None]
    return (new_max, new_sum, new_out)


def join_pair(mine, partner, ctx_index, bit_index):
    upper = ctx_index // 2**bit_index % 2 == 1
    joined = []
    for mine_part, other_part in zip(mine, partner):
        joined.append(
            jnp.where(
                upper,
                jnp.concatenate([other_part, mine_part], 0),
                jnp.concatenate([mine_part, other_part], 0),
            )
        )
    return tuple(joined)


def body(queries, keys, values, offsets, out_weight):
    rows_here = queries.shape[0]
    head_count = lax.axis_size("head")
    heads_here = offsets.shape[1] // head_count
    query_heads = queries.reshape(rows_here, heads_here, DH)
    key_heads = keys.reshape(rows_here, heads_here, DH)
    value_heads = values.reshape(rows_here, heads_here, DH)
    ctx_index = lax.axis_index("ctx")
    shifts_here = lax.dynamic_slice_in_dim(
        offsets, lax.axis_index("head") * heads_here, heads_here, 1
    )
    running = block_attend(query_heads, key_heads, value_heads, jnp.arange(rows_here))
    group = (key_heads, value_heads)
    sources = []
    for bit_index in range(LEVELS - 1):
        partner = swapped((group[0], group[1]), "ctx", bit_index)
        group = join_pair(group, partner, ctx_index, bit_index)
        dilation = 2 ** (bit_index + 1)
        sources.append(
            (
                pick_rows(group[0], shifts_here[bit_index], dilation),
                pick_rows(group[1], shifts_here[bit_index], dilation),
            )
        )
    for level_index in range(1, LEVELS):
        dilation = 2**level_index
        shifts_now = shifts_here[level_index - 1]
        query_rows = pick_rows(query_heads, shifts_now, dilation)
        span = rows_here // dilation
        query_pos = ctx_index % dilation * span + jnp.arange(span)
        parts = block_attend(
            query_rows, sources[level_index - 1][0], sources[level_index - 1][1], query_pos
        )
        running = merge_levels(running, spread_rows(parts, shifts_now, dilation))
    attended = (
        (running[2] / running[1][:, :, None])
        .astype(jnp.bfloat16)
        .reshape(rows_here, heads_here * DH)
    )
    regrouped = lax.all_to_all(attended, "head", split_axis=0, concat_axis=1, tiled=True)
    mixed = jnp.dot(regrouped, out_weight, preferred_element_type=jnp.float32)
    return mixed.astype(jnp.bfloat16)


def solution(mesh):
    placed = (P("ctx", "head"), P("ctx", "head"), P("ctx", "head"), P(), P())
    return jax.shard_map(
        body, mesh=mesh, in_specs=placed, out_specs=P(("ctx", "head"), None), check_vma=False
    )
```

profile of v0, /device:TPU:0, one launch (start us, length us, event | category | flops | bytes accessed | tf_op | source)
XLA Modules:
  0.0 672.1 jit_solution(2948327554374246019)
XLA Ops:
  22.7 45.2 %while.3 = (s32[]{:T(128)}, f32[3,512,4]{1,2,0:T(4,128)S(1)}, f32[3,512,4]{1,2,0:T(4,128)}, f32[3,512,4,128]{3,2,1,0:T(4,128)}, s32[3,512]{1,0:T(4,128)S(1)}, /*...) while((s32[]{:T(128)}, f32[3,512,4]{1,2,0:T(4,128)S(1)}, ...), condition=%wide.region_3.4_spmd.clone, body=%wide.region_0.3_spmd.clone.sunk | while | flops 1645998080 | bytes 48830580 | solution.py:52
  91.7 5.8 broadcast_in_dim.426
  100.7 6.7 broadcast_in_dim.441
  137.6 42.4 %fusion.32 = (bf16[1536,4,128]{2,0,1:T(8,128)(2,1)S(1)}, bf16[1536,4,128]{2,0,1:T(8,128)(2,1)S(1)}) fusion(bf16[1536,2,4,128]{3,1,0,2:T(2,128)(2,1)} %bitcast.100, pred[2,4]{0,1:T(4,128)(4,1)S(1)} %copy-done.28, bf16[1536,2,4,128]{3,1,0,2:T(2,128)(2,1)} %bitcast.101), kind=kLoop, calls=%fused_computation.52 | loop fusion | flops 4718592 | bytes 9437192 | tf_op jit(solution)/shard_map/reduce_sum | solution.py:21
  180.1 8.7 %fusion.14 = (f32[4,768]{1,0:T(4,128)S(1)}, f32[4,768,1536]{2,1,0:T(8,128)}) fusion(pred[768,1536]{1,0:T(8,128)(4,1)S(1)} %copy-done.5, bf16[1536,4,128]{2,0,1:T(8,128)(2,1)S(1)} %get-tuple-element.181, bf16[768,4,128]{2,1,0:T(4,128)(2,1)S(1)} %copy-done.10), kind=kOutput, calls=%fused_computation.21 | convolution fusion | flops 1222112256 | bytes 22425600 | tf_op jit(solution)/shard_map/while/body/eval_jaxpr/qhd,khd->hqk/dot_general | solution.py:36
  188.7 7.1 %maximum_select_fusion.3 = bf16[6144,4,128]{0,2,1:T(8,128)(2,1)} fusion(bf16[3072,4,128]{0,2,1:T(8,128)(2,1)S(1)} %maximum_select_fusion.5, bf16[3072,4,128]{0,2,1:T(8,128)(2,1)} %collective-permute-done.3, pred[]{:T(512)S(6)} %eq.62), kind=kLoop, calls=%fused_computation.38 | loop fusion | flops 28311552 | bytes 12582913 | tf_op jit(solution)/shard_map/jit(_where)/select_n | solution.py:87
  199.1 10.6 %fusion.40 = f32[768,4,128]{0,2,1:T(8,128)} fusion(bf16[1536,4,128]{2,0,1:T(8,128)(2,1)S(1)} %get-tuple-element.180, f32[4,768,1536]{2,1,0:T(8,128)} %get-tuple-element.221, f32[4,768]{1,0:T(4,128)S(1)} %get-tuple-element.220, pred[768,1536]{1,0:T(8,128)(4,1)S(1)} %copy-done.5), kind=kOutput, calls=%fused_computation.67 | convolution fusion | flops 1226833920 | bytes 23212032 | tf_op jit(solution)/shard_map/while/body/eval_jaxpr/hqk,khd->qhd/dot_general | solution.py:43
  213.4 10.6 %collective-permute-done.2 = bf16[3072,4,128]{0,2,1:T(8,128)(2,1)} collective-permute-done((bf16[3072,4,128]{0,2,1:T(8,128)(2,1)}, bf16[3072,4,128]{0,2,1:T(8,128)(2,1)}, u32[]{:S(2)}, u32[]{:S(2)}) %collective-permute-start.2) | collective-permute-done | bytes 3145760 | tf_op jit(solution)/shard_map/ppermute | solution.py:15
  224.0 7.1 %maximum_select_fusion.2 = bf16[6144,4,128]{0,2,1:T(8,128)(2,1)} fusion(bf16[3072,4,128]{0,2,1:T(8,128)(2,1)S(1)} %copy-done.3, bf16[3072,4,128]{0,2,1:T(8,128)(2,1)} %collective-permute-done.2, pred[]{:T(512)S(6)} %eq.62), kind=kLoop, calls=%fused_computation.37 | loop fusion | flops 28311552 | bytes 12582913 | tf_op jit(solution)/shard_map/jit(_where)/select_n | solution.py:87
  234.4 9.2 %fusion.15 = f32[4,768]{1,0:T(4,128)S(1)} fusion(f32[4,768,1536]{2,1,0:T(8,128)} %get-tuple-element.221, f32[4,768]{1,0:T(4,128)S(1)} %get-tuple-element.220, pred[768,1536]{1,0:T(8,128)(4,1)S(1)} %copy-done.6), kind=kLoop, calls=%fused_computation.22 | loop fusion | flops 18871296 | bytes 20078592 | tf_op jit(solution)/shard_map/while/body/eval_jaxpr/reduce_sum | solution.py:42
  250.7 8.7 %copy.92 = bf16[6144,4,128]{2,0,1:T(8,128)(2,1)} copy(bf16[6144,4,128]{0,2,1:T(8,128)(2,1)} %maximum_select_fusion.3) | data formatting | bytes 12582912 | tf_op jit(solution)/shard_map/jit(_where)/select_n | solution.py:87
  259.4 8.6 %copy.88 = bf16[6144,4,128]{2,0,1:T(8,128)(2,1)} copy(bf16[6144,4,128]{0,2,1:T(8,128)(2,1)} %maximum_select_fusion.2) | data formatting | bytes 12582912 | tf_op jit(solution)/shard_map/jit(_where)/select_n | solution.py:87
  268.0 42.8 %select_reduce_fusion = (bf16[1536,4,128]{2,0,1:T(8,128)(2,1)S(1)}, bf16[1536,4,128]{2,0,1:T(8,128)(2,1)S(1)}) fusion(bf16[1536,4,4,128]{3,1,0,2:T(4,128)(2,1)} %bitcast.97, pred[4,4]{0,1:T(4,128)(4,1)S(1)} %copy-done.26, bf16[1536,4,4,128]{3,1,0,2:T(4,128)(2,1)} %bitcast.98), kind=kLoop, calls=%fused_computation.39 | loop fusion | flops 11010048 | bytes 15728656 | tf_op jit(solution)/shard_map/reduce_sum | solution.py:21
  324.2 6.4 fusion.23
  336.3 25.0 %collective-permute-done.5 = bf16[6144,4,128]{0,2,1:T(8,128)(2,1)} collective-permute-done((bf16[6144,4,128]{0,2,1:T(8,128)(2,1)}, bf16[6144,4,128]{0,2,1:T(8,128)(2,1)}, u32[]{:S(2)}, u32[]{:S(2)}) %collective-permute-start.5) | collective-permute-done | bytes 6291488 | tf_op jit(solution)/shard_map/ppermute | solution.py:15
  361.4 15.6 %maximum_select_fusion.1 = bf16[12288,4,128]{0,2,1:T(8,128)(2,1)} fusion(bf16[6144,4,128]{0,2,1:T(8,128)(2,1)} %maximum_select_fusion.3, bf16[6144,4,128]{0,2,1:T(8,128)(2,1)} %collective-permute-done.5, pred[]{:T(512)S(6)} %eq.66), kind=kLoop, calls=%fused_computation.25 | loop fusion | flops 56623104 | bytes 25165824 | tf_op jit(solution)/shard_map/jit(_where)/select_n | solution.py:87
  377.0 16.6 %copy.100 = bf16[12288,4,128]{2,0,1:T(8,128)(2,1)} copy(bf16[12288,4,128]{0,2,1:T(8,128)(2,1)} %maximum_select_fusion.1) | data formatting | bytes 25165824 | tf_op jit(solution)/shard_map/jit(_where)/select_n | solution.py:87
  393.6 101.6 %collective-permute-done.4 = bf16[6144,4,128]{0,2,1:T(8,128)(2,1)} collective-permute-done((bf16[6144,4,128]{0,2,1:T(8,128)(2,1)}, bf16[6144,4,128]{0,2,1:T(8,128)(2,1)}, u32[]{:S(2)}, u32[]{:S(2)}) %collective-permute-start.4) | collective-permute-done | bytes 6291488 | tf_op jit(solution)/shard_map/ppermute | solution.py:15
  495.3 15.5 %maximum_select_fusion = bf16[12288,4,128]{0,2,1:T(8,128)(2,1)} fusion(bf16[6144,4,128]{0,2,1:T(8,128)(2,1)} %maximum_select_fusion.2, bf16[6144,4,128]{0,2,1:T(8,128)(2,1)} %collective-permute-done.4, pred[]{:T(512)S(6)} %eq.66), kind=kLoop, calls=%fused_computation.24 | loop fusion | flops 56623104 | bytes 25165824 | tf_op jit(solution)/shard_map/jit(_where)/select_n | solution.py:87
  510.8 16.6 %copy.96 = bf16[12288,4,128]{2,0,1:T(8,128)(2,1)} copy(bf16[12288,4,128]{0,2,1:T(8,128)(2,1)} %maximum_select_fusion) | data formatting | bytes 25165824 | tf_op jit(solution)/shard_map/jit(_where)/select_n | solution.py:87
  527.3 38.2 %fusion.17 = (bf16[1536,4,128]{2,0,1:T(8,128)(2,1)S(1)}, bf16[1536,4,128]{2,0,1:T(8,128)(2,1)S(1)}) fusion(bf16[12288,4,128]{2,0,1:T(8,128)(2,1)} %copy.100, pred[8,4]{0,1:T(4,128)(4,1)S(1)} %iota_compare_fusion.4, bf16[12288,4,128]{2,0,1:T(8,128)(2,1)} %copy.96), kind=kLoop, calls=%fused_computation.27 | loop fusion | flops 23592960 | bytes 28311584 | tf_op jit(solution)/shard_map/reduce_sum | solution.py:21
  627.8 10.9 %divide_convert_fusion = bf16[4,384,512]{2,1,0:T(8,128)(2,1)S(1)} fusion(f32[4,384,512]{2,1,0:T(8,128)} %div.35, f32[4,384,512]{2,1,0:T(8,128)} %mul.164, pred[4,384,512]{2,1,0:T(8,128)(4,1)} %broadcast_in_dim.456, f32[4,384,512]{2,1,0:T(8,128)S(1)} %bitcast.99, f32[4,384,512]{2,1,0:T(8,128)} %mul.161, f32[4,384,512]{2,1,0:T(8,128)} %mul.156, ...), kind=kLoop, calls=%fused_computation.55 | loop fusion | flops 11010048 | bytes 38535168 | tf_op jit(solution)/shard_map/convert_element_type | solution.py:132
  638.8 24.1 %all_to_all.16 = bf16[4,384,512]{2,1,0:T(8,128)(2,1)S(1)} all-to-all(bf16[4,384,512]{2,1,0:T(8,128)(2,1)S(1)} %divide_convert_fusion), channel_id=1, replica_groups=mesh['ctx'=32,'head'=4] {'head'}, dimensions={0} | all-to-all | bytes 3145728 | tf_op jit(solution)/shard_map/all_to_all | solution.py:135
  663.8 8.1 %convolution_convert_fusion = bf16[384,2048]{1,0:T(8,128)(2,1)} fusion(bf16[384,2048]{0,1:T(8,128)(2,1)S(1)} %bitcast.105, bf16[2048,2048]{1,0:T(8,128)(2,1)} %param.11), kind=kOutput, calls=%fused_computation.56 | convolution fusion | flops 3222011904 | bytes 11534336 | tf_op jit(solution)/shard_map/dot_general | solution.py:136
  (188 shorter events, 224.1 us)
Async XLA Ops:
  0.0 20.9 %copy-start = (s32[3,16]{1,0:T(4,128)S(1)}, s32[3,16]{1,0:T(4,128)}, u32[]{:S(2)}) copy-start(s32[3,16]{1,0:T(4,128)} %param.10) | copy-start | bytes 580
  2.6 78.9 %collective-permute-start.1 = (bf16[1536,4,128]{0,2,1:T(8,128)(2,1)}, bf16[1536,4,128]{0,2,1:T(8,128)(2,1)}, u32[]{:S(2)}, u32[]{:S(2)}) collective-permute-start(bf16[1536,4,128]{0,2,1:T(8,128)(2,1)} %bitcast.1), channel_id=1, source_target_pairs={{0,4},{4,0},{8,12},{12,8},{16,20},{20,16},{24,28},{28,24},{32,36},... | collective-permute-start | bytes 4718600 | tf_op jit(solution)/shard_map/ppermute | solution.py:15
  5.2 122.3 %collective-permute-start = (bf16[1536,4,128]{0,2,1:T(8,128)(2,1)}, bf16[1536,4,128]{0,2,1:T(8,128)(2,1)}, u32[]{:S(2)}, u32[]{:S(2)}) collective-permute-start(bf16[1536,4,128]{0,2,1:T(8,128)(2,1)} %bitcast), channel_id=1, source_target_pairs={{0,4},{4,0},{8,12},{12,8},{16,20},{20,16},{24,28},{28,24},{32,36},... | collective-permute-start | bytes 4718600 | tf_op jit(solution)/shard_map/ppermute | solution.py:15
  21.2 65.9 %copy-start.25 = (pred[4,4]{0,1:T(4,128)(4,1)}, pred[4,4]{0,1:T(4,128)(4,1)S(1)}, u32[]{:S(2)}) copy-start(pred[4,4]{0,1:T(4,128)(4,1)S(1)} %iota_compare_fusion.5) | copy-start | bytes 52
  68.0 17.5 %copy-start.23 = (f32[3,512,4]{1,2,0:T(4,128)}, f32[3,512,4]{1,2,0:T(4,128)S(1)}, u32[]{:S(2)}) copy-start(f32[3,512,4]{1,2,0:T(4,128)S(1)} %get-tuple-element.116) | copy-start | bytes 73732
  68.0 9.8 %copy-start.4 = (bf16[1536,512]{1,0:T(8,128)(2,1)S(1)}, bf16[1536,512]{1,0:T(8,128)(2,1)}, u32[]{:S(2)}) copy-start(bf16[1536,512]{1,0:T(8,128)(2,1)} %param.7) | copy-start | bytes 4718596
  77.8 10.9 %copy-start.28 = (pred[2,4]{0,1:T(4,128)(4,1)S(1)}, pred[2,4]{0,1:T(4,128)(4,1)}, u32[]{:S(2)}) copy-start(pred[2,4]{0,1:T(4,128)(4,1)} %copy-done.27) | copy-start | bytes 28
  85.4 103.3 %collective-permute-start.3 = (bf16[3072,4,128]{0,2,1:T(8,128)(2,1)S(1)}, bf16[3072,4,128]{0,2,1:T(8,128)(2,1)}, u32[]{:S(2)}, u32[]{:S(2)}) collective-permute-start(bf16[3072,4,128]{0,2,1:T(8,128)(2,1)S(1)} %maximum_select_fusion.5), channel_id=1, source_target_pairs={{0,8},{4,12},{8,0},{12,4},{16,24},{20,28},{24,16},{28,20},{32,40},... | collective-permute-start | bytes 9437192 | tf_op jit(solution)/shard_map/ppermute | solution.py:15
  90.6 19.9 %copy-start.14 = (pred[1536,4]{1,0:T(8,128)(4,1)S(1)}, pred[1536,4]{1,0:T(8,128)(4,1)}, u32[]{:S(2)}) copy-start(pred[1536,4]{1,0:T(8,128)(4,1)} %copy.99) | copy-start | bytes 18436
  110.5 14.0 %copy-start.29 = (s32[192]{0:T(256)S(1)}, s32[192]{0:T(256)}, u32[]{:S(2)}) copy-start(s32[192]{0:T(256)} %iota_add_fusion.2) | copy-start | bytes 2308
  137.2 86.8 %collective-permute-start.2 = (bf16[3072,4,128]{0,2,1:T(8,128)(2,1)}, bf16[3072,4,128]{0,2,1:T(8,128)(2,1)}, u32[]{:S(2)}, u32[]{:S(2)}) collective-permute-start(bf16[3072,4,128]{0,2,1:T(8,128)(2,1)} %maximum_select_fusion.4), channel_id=1, source_target_pairs={{0,8},{4,12},{8,0},{12,4},{16,24},{20,28},{24,16},{28,20},{32,40},... | collective-permute-start | bytes 9437192 | tf_op jit(solution)/shard_map/ppermute | solution.py:15
  137.6 42.4 %copy-start.5 = (pred[768,1536]{1,0:T(8,128)(4,1)S(1)}, pred[768,1536]{1,0:T(8,128)(4,1)}, u32[]{:S(2)}) copy-start(pred[768,1536]{1,0:T(8,128)(4,1)} %iota_compare_fusion.1) | copy-start | bytes 3538948
  137.6 42.5 %copy-start.10 = (bf16[768,4,128]{2,1,0:T(4,128)(2,1)S(1)}, bf16[768,4,128]{2,1,0:T(4,128)(2,1)}, u32[]{:S(2)}) copy-start(bf16[768,4,128]{2,1,0:T(4,128)(2,1)} %select_reduce_fusion.3) | copy-start | bytes 2359300
  195.8 165.6 %collective-permute-start.5 = (bf16[6144,4,128]{0,2,1:T(8,128)(2,1)}, bf16[6144,4,128]{0,2,1:T(8,128)(2,1)}, u32[]{:S(2)}, u32[]{:S(2)}) collective-permute-start(bf16[6144,4,128]{0,2,1:T(8,128)(2,1)} %maximum_select_fusion.3), channel_id=1, source_target_pairs={{0,16},{4,20},{8,24},{12,28},{16,0},{20,4},{24,8},{28,12},{32,48},... | collective-permute-start | bytes 18874376 | tf_op jit(solution)/shard_map/ppermute | solution.py:15
  209.7 14.2 %copy-start.3 = (bf16[3072,4,128]{0,2,1:T(8,128)(2,1)S(1)}, bf16[3072,4,128]{0,2,1:T(8,128)(2,1)}, u32[]{:S(2)}) copy-start(bf16[3072,4,128]{0,2,1:T(8,128)(2,1)} %maximum_select_fusion.4) | copy-start | bytes 9437188
  213.4 21.0 %copy-start.6 = (pred[768,1536]{1,0:T(8,128)(4,1)S(1)}, pred[768,1536]{1,0:T(8,128)(4,1)}, u32[]{:S(2)}) copy-start(pred[768,1536]{1,0:T(8,128)(4,1)} %iota_compare_fusion.1) | copy-start | bytes 3538948
  231.1 13.9 %copy-start.12 = (f32[768,4]{1,0:T(8,128)S(1)}, f32[768,4]{1,0:T(8,128)}, u32[]{:S(2)}) copy-start(f32[768,4]{1,0:T(8,128)} %copy.79) | copy-start | bytes 36868
  231.1 264.2 %collective-permute-start.4 = (bf16[6144,4,128]{0,2,1:T(8,128)(2,1)}, bf16[6144,4,128]{0,2,1:T(8,128)(2,1)}, u32[]{:S(2)}, u32[]{:S(2)}) collective-permute-start(bf16[6144,4,128]{0,2,1:T(8,128)(2,1)} %maximum_select_fusion.2), channel_id=1, source_target_pairs={{0,16},{4,20},{8,24},{12,28},{16,0},{20,4},{24,8},{28,12},{32,48},... | collective-permute-start | bytes 18874376 | tf_op jit(solution)/shard_map/ppermute | solution.py:15
  259.4 8.6 %copy-start.26 = (pred[4,4]{0,1:T(4,128)(4,1)S(1)}, pred[4,4]{0,1:T(4,128)(4,1)}, u32[]{:S(2)}) copy-start(pred[4,4]{0,1:T(4,128)(4,1)} %copy-done.25) | copy-start | bytes 52
  268.0 42.8 %copy-start.9 = (pred[384,1536]{1,0:T(8,128)(4,1)S(1)}, pred[384,1536]{1,0:T(8,128)(4,1)}, u32[]{:S(2)}) copy-start(pred[384,1536]{1,0:T(8,128)(4,1)} %iota_compare_fusion.2) | copy-start | bytes 1769476
  268.0 42.8 %copy-start.11 = (bf16[384,4,128]{2,1,0:T(4,128)(2,1)S(1)}, bf16[384,4,128]{2,1,0:T(4,128)(2,1)}, u32[]{:S(2)}) copy-start(bf16[384,4,128]{2,1,0:T(4,128)(2,1)} %select_reduce_fusion.2) | copy-start | bytes 1179652
  527.3 38.2 %copy-start.13 = (bf16[192,4,128]{2,1,0:T(4,128)(2,1)S(1)}, bf16[192,4,128]{2,1,0:T(4,128)(2,1)}, u32[]{:S(2)}) copy-start(bf16[192,4,128]{2,1,0:T(4,128)(2,1)} %fusion.39) | copy-start | bytes 589828
  620.6 5.8 copy-start.7
  663.8 8.1 %copy-start.1 = (s32[3,16]{1,0:T(4,128)S(1)}, s32[3,16]{1,0:T(4,128)}, u32[]{:S(2)}) copy-start(s32[3,16]{1,0:T(4,128)} %param.10) | copy-start | bytes 580
  (12 other events, 29.0 us)
where the time goes:
time: 683 us; the launch traced here: 672 us
  other arithmetic  232 us (34%)
  local copies, waits for them, and re-layouts  210 us (31%)
  waiting for transfers between devices  137 us (20%)
  matrix products  58.1 us (9%)
  blocking collectives  24.1 us (4%)
  starting transfers between devices  9.23 us (1%)
    ppermute x6, waiting for transfers between devices, swapped(): return lax.ppermute(value, axis, pairs)  137 us
    reduce_sum x6, other arithmetic, pick_rows(): jnp.sum(jnp.where(hits[None, :, :, None], shaped, jnp.zeros((), source.dt...  133 us
    select_n x6, local copies, waits for them, and re-layouts, join_pair(): jnp.where(upper, jnp.concatenate([other_part, mine_part], 0), jnp.concate...  57.9 us
    select_n x6, other arithmetic, join_pair(): jnp.where(upper, jnp.concatenate([other_part, mine_part], 0), jnp.concate...  54.3 us
    dot_general x6, matrix products, one_block(): jnp.einsum('hqk,khd->qhd', weights.astype(jnp.bfloat16), value_rows, pref...  29.6 us
    reduce_sum x6, other arithmetic, one_block(): row_sum = jnp.sum(weights, axis=2)  27.9 us
    broadcast_in_dim x6, local copies, waits for them, and re-layouts, pick_rows(): jnp.where(hits[None, :, :, None], shaped, jnp.zeros((), source.dtype))  27.7 us
    all_to_all x1, blocking collectives, body(): lax.all_to_all(attended, 'head', split_axis=0, concat_axis=1, tiled=True)  24.1 us
  transfers between devices with their start and end apart: 6, of which 3 were waited for; matrix products, arithmetic and copies ran while one was open for 51% of the time, Pallas kernels for 0%

commit v1 on v0

--- a/solution.py
+++ b/solution.py
@@ -132,7 +132,10 @@
         .astype(jnp.bfloat16)
         .reshape(rows_here, heads_here * DH)
     )
-    regrouped = lax.all_to_all(attended, "head", split_axis=0, concat_axis=1, tiled=True)
+    regrouped = jnp.concatenate(
+        lax.all_to_all(jnp.stack(jnp.split(attended, lax.axis_size("head"), axis=0)), "head", 0, 0),
+        axis=1,
+    )
     mixed = jnp.dot(regrouped, out_weight, preferred_element_type=jnp.float32)
     return mixed.astype(jnp.bfloat16)
 

time: 683 us -> 624 us (0.914)
  local copies, waits for them, and re-layouts: 210 us -> 103 us
  waiting for transfers between devices: 137 us -> 183 us
    ppermute x6, waiting for transfers between devices: 137 us -> 183 us  [swapped(): return lax.ppermute(value, axis, pairs)]
    mul x12 -> x0, local copies, waits for them, and re-layouts: 37 us -> none  [the longest x6 18.6 us: merge_levels(): fresh[2] * new_scale[:, :, None]]
    broadcast_in_dim x6 -> x0, local copies, waits for them, and re-layouts: 27.7 us -> none  [pick_rows(): jnp.where(hits[None, :, :, None], shaped, jnp.zeros((), source.dtype))]
    div x2 -> x0, local copies, waits for them, and re-layouts: 9.62 us -> none  [body(): running[2] / running[1][:, :, None]]
    broadcast_in_dim x5 -> x2, local copies, waits for them, and re-layouts: 9.43 us -> 1.62 us  [spread_rows(): jnp.where(hits[None, :, :, None], weighted[:, None], 0.0)]
    exp x6 -> x0, local copies, waits for them, and re-layouts: 7.17 us -> none  [the longest x3 3.59 us: merge_levels(): old_scale = jnp.exp(running[0] - new_max)]
    unnamed x64 -> x46, local copies, waits for them, and re-layouts: 15 us -> 13.9 us
  transfers between devices with their start and end apart: 6 -> 6, of which waited for: 3 -> 4; matrix products, arithmetic and copies ran while one was open for 51% -> 48% of each run, Pallas kernels for 0% -> 0%
where the time goes in v1:
time: 624 us; the launch traced here: 615 us
  other arithmetic  232 us (37%)
  waiting for transfers between devices  183 us (29%)
  local copies, waits for them, and re-layouts  103 us (17%)
  matrix products  62.3 us (10%)
  blocking collectives  24.1 us (4%)
  starting transfers between devices  9.23 us (1%)
    ppermute x6, waiting for transfers between devices, swapped(): return lax.ppermute(value, axis, pairs)  183 us
    reduce_sum x6, other arithmetic, pick_rows(): jnp.sum(jnp.where(hits[None, :, :, None], shaped, jnp.zeros((), source.dt...  133 us
    select_n x6, local copies, waits for them, and re-layouts, join_pair(): jnp.where(upper, jnp.concatenate([other_part, mine_part], 0), jnp.concate...  58 us
    select_n x6, other arithmetic, join_pair(): jnp.where(upper, jnp.concatenate([other_part, mine_part], 0), jnp.concate...  54.1 us
    dot_general x6, matrix products, one_block(): jnp.einsum('hqk,khd->qhd', weights.astype(jnp.bfloat16), value_rows, pref...  33.8 us
    reduce_sum x6, other arithmetic, one_block(): row_sum = jnp.sum(weights, axis=2)  28.3 us
    all_to_all x1, blocking collectives, body(): lax.all_to_all(jnp.stack(jnp.split(attended, lax.axis_size('head'), axis=...  24.1 us
    dot_general x6, matrix products, one_block(): jnp.einsum('qhd,khd->hqk', rows_now, key_rows, preferred_element_type=jnp...  20.5 us
  transfers between devices with their start and end apart: 6, of which 4 were waited for; matrix products, arithmetic and copies ran while one was open for 48% of the time, Pallas kernels for 0%

profile of v1, /device:TPU:0, one launch (start us, length us, event | category | flops | bytes accessed | tf_op | source)
XLA Modules:
  0.0 614.9 jit_solution(4922505340865720858)
XLA Ops:
  21.8 44.8 %while.3 = (s32[]{:T(128)}, f32[3,512,4]{1,2,0:T(4,128)S(1)}, f32[3,512,4]{1,2,0:T(4,128)}, f32[3,512,4,128]{3,1,0,2:T(8,128)}, s32[3,512]{1,0:T(4,128)S(1)}, /*...) while((s32[]{:T(128)}, f32[3,512,4]{1,2,0:T(4,128)S(1)}, ...), condition=%wide.region_3.4_spmd.clone, body=%wide.region_0.3_spmd.clone.sunk | while | flops 1645998080 | bytes 46733428 | solution.py:52
  44.8 6.0 fusion.98
  59.6 6.0 fusion.98
  102.6 42.2 %fusion.34 = (bf16[1536,4,128]{2,0,1:T(8,128)(2,1)S(1)}, bf16[1536,4,128]{2,0,1:T(8,128)(2,1)S(1)}) fusion(bf16[1536,2,4,128]{3,1,0,2:T(2,128)(2,1)} %bitcast.135, pred[2,4]{0,1:T(4,128)(4,1)S(1)} %copy-done.20, bf16[1536,2,4,128]{3,1,0,2:T(2,128)(2,1)} %bitcast.133), kind=kLoop, calls=%fused_computation.51 | loop fusion | flops 4718592 | bytes 9437192 | tf_op jit(solution)/shard_map/reduce_sum | solution.py:21
  144.8 8.7 %fusion.17 = (f32[4,768]{1,0:T(4,128)S(1)}, f32[4,768,1536]{2,1,0:T(8,128)}) fusion(pred[768,1536]{1,0:T(8,128)(4,1)S(1)} %copy-done.5, bf16[1536,4,128]{2,0,1:T(8,128)(2,1)S(1)} %get-tuple-element.182, bf16[768,4,128]{2,1,0:T(4,128)(2,1)S(1)} %copy-done.9), kind=kOutput, calls=%fused_computation.21 | convolution fusion | flops 1222112256 | bytes 22425600 | tf_op jit(solution)/shard_map/while/body/eval_jaxpr/qhd,khd->hqk/dot_general | solution.py:36
  155.0 7.1 %maximum_select_fusion.3 = bf16[6144,4,128]{0,2,1:T(8,128)(2,1)} fusion(bf16[3072,4,128]{0,2,1:T(8,128)(2,1)S(1)} %maximum_select_fusion.5, bf16[3072,4,128]{0,2,1:T(8,128)(2,1)} %collective-permute-done.3, pred[]{:T(512)S(6)} %eq.62), kind=kLoop, calls=%fused_computation.38 | loop fusion | flops 28311552 | bytes 12582913 | tf_op jit(solution)/shard_map/jit(_where)/select_n | solution.py:87
  165.3 10.4 %fusion.51 = f32[768,4,128]{0,2,1:T(8,128)} fusion(bf16[1536,4,128]{2,0,1:T(8,128)(2,1)S(1)} %get-tuple-element.183, f32[4,768,1536]{2,1,0:T(8,128)} %get-tuple-element.223, f32[4,768]{1,0:T(4,128)S(1)} %get-tuple-element.222, pred[768,1536]{1,0:T(8,128)(4,1)S(1)} %copy-done.5), kind=kOutput, calls=%fused_computation.77 | convolution fusion | flops 1226833920 | bytes 23212032 | tf_op jit(solution)/shard_map/while/body/eval_jaxpr/hqk,khd->qhd/dot_general | solution.py:43
  180.0 42.4 %collective-permute-done.2 = bf16[3072,4,128]{0,2,1:T(8,128)(2,1)} collective-permute-done((bf16[3072,4,128]{0,2,1:T(8,128)(2,1)}, bf16[3072,4,128]{0,2,1:T(8,128)(2,1)}, u32[]{:S(2)}, u32[]{:S(2)}) %collective-permute-start.2) | collective-permute-done | bytes 3145760 | tf_op jit(solution)/shard_map/ppermute | solution.py:15
  222.4 7.1 %maximum_select_fusion.2 = bf16[6144,4,128]{0,2,1:T(8,128)(2,1)} fusion(bf16[3072,4,128]{0,2,1:T(8,128)(2,1)S(1)} %copy-done.3, bf16[3072,4,128]{0,2,1:T(8,128)(2,1)} %collective-permute-done.2, pred[]{:T(512)S(6)} %eq.62), kind=kLoop, calls=%fused_computation.37 | loop fusion | flops 28311552 | bytes 12582913 | tf_op jit(solution)/shard_map/jit(_where)/select_n | solution.py:87
  232.8 9.6 %fusion.18 = f32[4,768]{1,0:T(4,128)S(1)} fusion(f32[4,768,1536]{2,1,0:T(8,128)} %get-tuple-element.223, f32[4,768]{1,0:T(4,128)S(1)} %get-tuple-element.222, pred[768,1536]{1,0:T(8,128)(4,1)S(1)} %copy-done.6), kind=kLoop, calls=%fused_computation.22 | loop fusion | flops 18871296 | bytes 20078592 | tf_op jit(solution)/shard_map/while/body/eval_jaxpr/reduce_sum | solution.py:42
  243.7 8.6 %copy.67 = bf16[6144,4,128]{2,0,1:T(8,128)(2,1)} copy(bf16[6144,4,128]{0,2,1:T(8,128)(2,1)} %maximum_select_fusion.3) | data formatting | bytes 12582912 | tf_op jit(solution)/shard_map/jit(_where)/select_n | solution.py:87
  252.3 8.7 %copy.65 = bf16[6144,4,128]{2,0,1:T(8,128)(2,1)} copy(bf16[6144,4,128]{0,2,1:T(8,128)(2,1)} %maximum_select_fusion.2) | data formatting | bytes 12582912 | tf_op jit(solution)/shard_map/jit(_where)/select_n | solution.py:87
  261.0 42.6 %select_reduce_fusion.1 = (bf16[1536,4,128]{2,0,1:T(8,128)(2,1)S(1)}, bf16[1536,4,128]{2,0,1:T(8,128)(2,1)S(1)}) fusion(bf16[1536,4,4,128]{3,1,0,2:T(4,128)(2,1)} %bitcast.132, pred[4,4]{0,1:T(4,128)(4,1)S(1)} %copy-done.18, bf16[1536,4,4,128]{3,1,0,2:T(4,128)(2,1)} %bitcast.131), kind=kLoop, calls=%fused_computation.40 | loop fusion | flops 11010048 | bytes 15728656 | tf_op jit(solution)/shard_map/reduce_sum | solution.py:21
  315.4 6.4 %fusion.26 = f32[4,384]{1,0:T(4,128)S(1)} fusion(f32[4,384,1536]{2,1,0:T(8,128)} %copy-done.2, f32[4,384]{1,0:T(4,128)S(1)} %get-tuple-element.220, pred[384,1536]{1,0:T(8,128)(4,1)S(1)} %copy-done.8), kind=kLoop, calls=%fused_computation.35 | loop fusion | flops 9435648 | bytes 10039296 | tf_op jit(solution)/shard_map/while/body/eval_jaxpr/reduce_sum | solution.py:42
  322.6 37.2 %collective-permute-done.5 = bf16[6144,4,128]{0,2,1:T(8,128)(2,1)} collective-permute-done((bf16[6144,4,128]{0,2,1:T(8,128)(2,1)}, bf16[6144,4,128]{0,2,1:T(8,128)(2,1)}, u32[]{:S(2)}, u32[]{:S(2)}) %collective-permute-start.5) | collective-permute-done | bytes 6291488 | tf_op jit(solution)/shard_map/ppermute | solution.py:15
  359.8 15.5 %maximum_select_fusion.1 = bf16[12288,4,128]{0,2,1:T(8,128)(2,1)} fusion(bf16[6144,4,128]{0,2,1:T(8,128)(2,1)} %maximum_select_fusion.3, bf16[6144,4,128]{0,2,1:T(8,128)(2,1)} %collective-permute-done.5, pred[]{:T(512)S(6)} %eq.66), kind=kLoop, calls=%fused_computation.25 | loop fusion | flops 56623104 | bytes 25165824 | tf_op jit(solution)/shard_map/jit(_where)/select_n | solution.py:87
  375.3 16.6 %copy.72 = bf16[12288,4,128]{2,0,1:T(8,128)(2,1)} copy(bf16[12288,4,128]{0,2,1:T(8,128)(2,1)} %maximum_select_fusion.1) | data formatting | bytes 25165824 | tf_op jit(solution)/shard_map/jit(_where)/select_n | solution.py:87
  391.9 101.8 %collective-permute-done.4 = bf16[6144,4,128]{0,2,1:T(8,128)(2,1)} collective-permute-done((bf16[6144,4,128]{0,2,1:T(8,128)(2,1)}, bf16[6144,4,128]{0,2,1:T(8,128)(2,1)}, u32[]{:S(2)}, u32[]{:S(2)}) %collective-permute-start.4) | collective-permute-done | bytes 6291488 | tf_op jit(solution)/shard_map/ppermute | solution.py:15
  493.6 15.6 %maximum_select_fusion = bf16[12288,4,128]{0,2,1:T(8,128)(2,1)} fusion(bf16[6144,4,128]{0,2,1:T(8,128)(2,1)} %maximum_select_fusion.2, bf16[6144,4,128]{0,2,1:T(8,128)(2,1)} %collective-permute-done.4, pred[]{:T(512)S(6)} %eq.66), kind=kLoop, calls=%fused_computation.24 | loop fusion | flops 56623104 | bytes 25165824 | tf_op jit(solution)/shard_map/jit(_where)/select_n | solution.py:87
  509.2 16.6 %copy.70 = bf16[12288,4,128]{2,0,1:T(8,128)(2,1)} copy(bf16[12288,4,128]{0,2,1:T(8,128)(2,1)} %maximum_select_fusion) | data formatting | bytes 25165824 | tf_op jit(solution)/shard_map/jit(_where)/select_n | solution.py:87
  525.8 38.3 %fusion.20 = (bf16[1536,4,128]{2,0,1:T(8,128)(2,1)S(1)}, bf16[1536,4,128]{2,0,1:T(8,128)(2,1)S(1)}) fusion(bf16[12288,4,128]{2,0,1:T(8,128)(2,1)} %copy.72, pred[8,4]{0,1:T(4,128)(4,1)S(1)} %iota_compare_fusion.4, bf16[12288,4,128]{2,0,1:T(8,128)(2,1)} %copy.70), kind=kLoop, calls=%fused_computation.27 | loop fusion | flops 23592960 | bytes 28311584 | tf_op jit(solution)/shard_map/reduce_sum | solution.py:21
  571.6 9.3 %fusion.43 = bf16[1536,4,128]{2,0,1:T(8,128)(2,1)S(1)} fusion(f32[1536,4,128]{2,0,1:T(8,128)S(1)} %bitcast.136, f32[1536,4,128]{2,0,1:T(8,128)S(1)} %bitcast.134, f32[3,512,4,128]{3,1,0,2:T(8,128)S(1)} %copy-done.10, f32[1536,4]{0,1:T(4,128)S(1)} %get-tuple-element.202, f32[1536,4]{0,1:T(4,128)S(1)} %get-tuple-element.208, f32[192,4,128]{2,0,1:T(8,128)S(1)} %fusion.57, ...), kind=kLoop, calls=%fused_computation.64 | loop fusion | flops 11010048 | bytes 11593728 | tf_op jit(solution)/shard_map/convert_element_type | solution.py:132
  582.3 24.1 %all_to_all.5 = bf16[4,384,512]{1,2,0:T(8,128)(2,1)S(1)} all-to-all(bf16[4,384,512]{1,2,0:T(8,128)(2,1)S(1)} %pad_maximum_fusion), channel_id=1, replica_groups=mesh['ctx'=32,'head'=4] {'head'}, dimensions={0} | all-to-all | bytes 3145728 | tf_op jit(solution)/shard_map/all_to_all | solution.py:136
  606.4 8.1 %convolution_convert_fusion = bf16[384,2048]{1,0:T(8,128)(2,1)} fusion(bf16[384,2048]{0,1:T(8,128)(2,1)S(1)} %bitcast.139, bf16[2048,2048]{1,0:T(8,128)(2,1)} %param.11), kind=kOutput, calls=%fused_computation.65 | convolution fusion | flops 3222011904 | bytes 11534336 | tf_op jit(solution)/shard_map/dot_general | solution.py:139
  (137 shorter events, 124.8 us)
Async XLA Ops:
  0.0 20.9 %copy-start = (s32[3,16]{1,0:T(4,128)S(1)}, s32[3,16]{1,0:T(4,128)}, u32[]{:S(2)}) copy-start(s32[3,16]{1,0:T(4,128)} %param.10) | copy-start | bytes 580
  2.6 77.5 %collective-permute-start.1 = (bf16[1536,4,128]{0,2,1:T(8,128)(2,1)}, bf16[1536,4,128]{0,2,1:T(8,128)(2,1)}, u32[]{:S(2)}, u32[]{:S(2)}) collective-permute-start(bf16[1536,4,128]{0,2,1:T(8,128)(2,1)} %bitcast.1), channel_id=1, source_target_pairs={{0,4},{4,0},{8,12},{12,8},{16,20},{20,16},{24,28},{28,24},{32,36},... | collective-permute-start | bytes 4718600 | tf_op jit(solution)/shard_map/ppermute | solution.py:15
  5.2 87.4 %collective-permute-start = (bf16[1536,4,128]{0,2,1:T(8,128)(2,1)}, bf16[1536,4,128]{0,2,1:T(8,128)(2,1)}, u32[]{:S(2)}, u32[]{:S(2)}) collective-permute-start(bf16[1536,4,128]{0,2,1:T(8,128)(2,1)} %bitcast), channel_id=1, source_target_pairs={{0,4},{4,0},{8,12},{12,8},{16,20},{20,16},{24,28},{28,24},{32,36},... | collective-permute-start | bytes 4718600 | tf_op jit(solution)/shard_map/ppermute | solution.py:15
  21.2 65.3 %copy-start.17 = (pred[4,4]{0,1:T(4,128)(4,1)}, pred[4,4]{0,1:T(4,128)(4,1)S(1)}, u32[]{:S(2)}) copy-start(pred[4,4]{0,1:T(4,128)(4,1)S(1)} %iota_compare_fusion.5) | copy-start | bytes 52
  66.6 13.4 %copy-start.16 = (f32[3,512,4]{1,2,0:T(4,128)}, f32[3,512,4]{1,2,0:T(4,128)S(1)}, u32[]{:S(2)}) copy-start(f32[3,512,4]{1,2,0:T(4,128)S(1)} %get-tuple-element.116) | copy-start | bytes 73732
  66.7 9.8 %copy-start.4 = (bf16[1536,512]{1,0:T(8,128)(2,1)S(1)}, bf16[1536,512]{1,0:T(8,128)(2,1)}, u32[]{:S(2)}) copy-start(bf16[1536,512]{1,0:T(8,128)(2,1)} %param.7) | copy-start | bytes 4718596
  76.4 10.6 %copy-start.20 = (pred[2,4]{0,1:T(4,128)(4,1)S(1)}, pred[2,4]{0,1:T(4,128)(4,1)}, u32[]{:S(2)}) copy-start(pred[2,4]{0,1:T(4,128)(4,1)} %copy-done.19) | copy-start | bytes 28
  83.8 71.2 %collective-permute-start.3 = (bf16[3072,4,128]{0,2,1:T(8,128)(2,1)S(1)}, bf16[3072,4,128]{0,2,1:T(8,128)(2,1)}, u32[]{:S(2)}, u32[]{:S(2)}) collective-permute-start(bf16[3072,4,128]{0,2,1:T(8,128)(2,1)S(1)} %maximum_select_fusion.5), channel_id=1, source_target_pairs={{0,8},{4,12},{8,0},{12,4},{16,24},{20,28},{24,16},{28,20},{32,40},... | collective-permute-start | bytes 9437192 | tf_op jit(solution)/shard_map/ppermute | solution.py:15
  102.2 120.1 %collective-permute-start.2 = (bf16[3072,4,128]{0,2,1:T(8,128)(2,1)}, bf16[3072,4,128]{0,2,1:T(8,128)(2,1)}, u32[]{:S(2)}, u32[]{:S(2)}) collective-permute-start(bf16[3072,4,128]{0,2,1:T(8,128)(2,1)} %maximum_select_fusion.4), channel_id=1, source_target_pairs={{0,8},{4,12},{8,0},{12,4},{16,24},{20,28},{24,16},{28,20},{32,40},... | collective-permute-start | bytes 9437192 | tf_op jit(solution)/shard_map/ppermute | solution.py:15
  102.6 42.2 %copy-start.5 = (pred[768,1536]{1,0:T(8,128)(4,1)S(1)}, pred[768,1536]{1,0:T(8,128)(4,1)}, u32[]{:S(2)}) copy-start(pred[768,1536]{1,0:T(8,128)(4,1)} %iota_compare_fusion.1) | copy-start | bytes 3538948
  102.6 42.2 %copy-start.9 = (bf16[768,4,128]{2,1,0:T(4,128)(2,1)S(1)}, bf16[768,4,128]{2,1,0:T(4,128)(2,1)}, u32[]{:S(2)}) copy-start(bf16[768,4,128]{2,1,0:T(4,128)(2,1)} %select_reduce_fusion.3) | copy-start | bytes 2359300
  162.0 197.7 %collective-permute-start.5 = (bf16[6144,4,128]{0,2,1:T(8,128)(2,1)}, bf16[6144,4,128]{0,2,1:T(8,128)(2,1)}, u32[]{:S(2)}, u32[]{:S(2)}) collective-permute-start(bf16[6144,4,128]{0,2,1:T(8,128)(2,1)} %maximum_select_fusion.3), channel_id=1, source_target_pairs={{0,16},{4,20},{8,24},{12,28},{16,0},{20,4},{24,8},{28,12},{32,48},... | collective-permute-start | bytes 18874376 | tf_op jit(solution)/shard_map/ppermute | solution.py:15
  175.8 46.6 %copy-start.3 = (bf16[3072,4,128]{0,2,1:T(8,128)(2,1)S(1)}, bf16[3072,4,128]{0,2,1:T(8,128)(2,1)}, u32[]{:S(2)}) copy-start(bf16[3072,4,128]{0,2,1:T(8,128)(2,1)} %maximum_select_fusion.4) | copy-start | bytes 9437188
  180.0 52.8 %copy-start.6 = (pred[768,1536]{1,0:T(8,128)(4,1)S(1)}, pred[768,1536]{1,0:T(8,128)(4,1)}, u32[]{:S(2)}) copy-start(pred[768,1536]{1,0:T(8,128)(4,1)} %iota_compare_fusion.1) | copy-start | bytes 3538948
  229.5 13.7 %copy-start.12 = (f32[768,4]{1,0:T(8,128)S(1)}, f32[768,4]{1,0:T(8,128)}, u32[]{:S(2)}) copy-start(f32[768,4]{1,0:T(8,128)} %copy.59) | copy-start | bytes 36868
  229.5 264.1 %collective-permute-start.4 = (bf16[6144,4,128]{0,2,1:T(8,128)(2,1)}, bf16[6144,4,128]{0,2,1:T(8,128)(2,1)}, u32[]{:S(2)}, u32[]{:S(2)}) collective-permute-start(bf16[6144,4,128]{0,2,1:T(8,128)(2,1)} %maximum_select_fusion.2), channel_id=1, source_target_pairs={{0,16},{4,20},{8,24},{12,28},{16,0},{20,4},{24,8},{28,12},{32,48},... | collective-permute-start | bytes 18874376 | tf_op jit(solution)/shard_map/ppermute | solution.py:15
  252.3 8.7 %copy-start.18 = (pred[4,4]{0,1:T(4,128)(4,1)S(1)}, pred[4,4]{0,1:T(4,128)(4,1)}, u32[]{:S(2)}) copy-start(pred[4,4]{0,1:T(4,128)(4,1)} %copy-done.17) | copy-start | bytes 52
  261.0 42.6 %copy-start.8 = (pred[384,1536]{1,0:T(8,128)(4,1)S(1)}, pred[384,1536]{1,0:T(8,128)(4,1)}, u32[]{:S(2)}) copy-start(pred[384,1536]{1,0:T(8,128)(4,1)} %iota_compare_fusion.2) | copy-start | bytes 1769476
  261.0 42.6 %copy-start.11 = (bf16[384,4,128]{2,1,0:T(4,128)(2,1)S(1)}, bf16[384,4,128]{2,1,0:T(4,128)(2,1)}, u32[]{:S(2)}) copy-start(bf16[384,4,128]{2,1,0:T(4,128)(2,1)} %select_reduce_fusion.2) | copy-start | bytes 1179652
  305.7 3.6 copy-start.2
  525.8 38.3 %copy-start.13 = (bf16[192,4,128]{2,1,0:T(4,128)(2,1)S(1)}, bf16[192,4,128]{2,1,0:T(4,128)(2,1)}, u32[]{:S(2)}) copy-start(bf16[192,4,128]{2,1,0:T(4,128)(2,1)} %fusion.50) | copy-start | bytes 589828
  568.7 2.9 copy-start.14
  568.7 2.9 copy-start.15
  606.4 8.1 %copy-start.1 = (s32[3,16]{1,0:T(4,128)S(1)}, s32[3,16]{1,0:T(4,128)}, u32[]{:S(2)}) copy-start(s32[3,16]{1,0:T(4,128)} %param.10) | copy-start | bytes 580
  (3 other events, 5.7 us)
